TPU v7x, 32 devices: a whole 2x2x4 slice. The times are simulated.
32 devices in a mesh: seq: 16 (over z, x, core), head: 2 (over y).
Axes of the slice: x: 2, y: 2, z: 4, core: 2. Of those that a mesh axis runs over, the one named last changes fastest.
Arguments:
- features: bfloat16 [8, 32, 8, 512], P(None, 'seq', 'head'), may hold values from -540 to 540
- gn_gain: float32 [512], replicated, may hold values from 0.5 to 1.5
- gn_bias: float32 [512], replicated, may hold values from -3 to 3
- conv_weight: bfloat16 [3, 3, 3, 16, 512], replicated, may hold values from -0.0546875 to 0.0546875
- conv_bias: float32 [16], replicated, may hold values from -3 to 3
- patch_weight: bfloat16 [64, 3072], replicated, may hold values from -0.75 to 0.75
- patch_bias: float32 [3072], replicated, may hold values from -3 to 3
- image_mod: float32 [3, 3072], replicated, may hold values from -3 to 3
- w_qkv: bfloat16 [3072, 3, 2048], P('seq', None, 'head'), may hold values from -5 to 5
- text_ids: int32 [512], replicated, may hold values from 0 to 16383
- text_length: int32 [1], replicated, may hold values from 256 to 512
- text_table: bfloat16 [3072, 16384], P('seq'), may hold values from -60 to 60
- text_mod: float32 [2, 3072], P(None, 'seq'), may hold values from -3 to 3
- w_text: bfloat16 [3072, 2, 2048], P('seq', None, 'head'), may hold values from -2 to 2
- w_out: bfloat16 [2048, 3072], P('head'), may hold values from -0.625 to 0.625
- out_bias: float32 [3072], replicated, may hold values from -3 to 3
Outputs:
- block_out: bfloat16 [8, 16, 4, 3072], P(None, 'seq', 'head')
All inputs are finite; a program needn't handle non-finite values.
Results may differ from a plain program's by a relative error of at most 0.0089.
Values may be sent and summed in bfloat16 or wider, within the bound.
A program may use at most 128 MiB of HBM per device.

v0:
```python
import jax
import jax.numpy as jnp
from jax import lax
from jax.sharding import PartitionSpec as P

HD = 128
GN_GROUPS = 32
CHUNK = 512
eps_norm = 1e-06


def group_gather(piece, group, dim):
    if group == 1:
        return piece
    count = lax.axis_size("seq")
    if group == 2:
        other = lax.ppermute(piece, "seq", [(i, i ^ 1) for i in range(count)])
        first = lax.axis_index("seq") % 2 == 0
        return jnp.concatenate(
            [jnp.where(first, piece, other), jnp.where(first, other, piece)], axis=dim
        )
    members = [list(range(i, i + group)) for i in range(0, count, group)]
    return lax.all_gather(piece, "seq", axis=dim, tiled=True, axis_index_groups=members)


def group_norm(features, gn_gain, gn_bias):
    frame_count, row_count, col_count, chan_count = features.shape
    per_group = chan_count // GN_GROUPS
    values = features.astype(jnp.float32)
    chan_sums = jnp.stack(
        [jnp.sum(values, axis=(0, 1, 2)), jnp.sum(values * values, axis=(0, 1, 2))]
    )
    sums = jnp.sum(chan_sums.reshape(2, GN_GROUPS, per_group), axis=2)
    sums = lax.psum(sums, ("seq", "head"))
    cell_count = (
        frame_count
        * row_count
        * col_count
        * per_group
        * lax.axis_size("seq")
        * lax.axis_size("head")
    )
    mean = sums[0] / cell_count
    scale = lax.rsqrt(sums[1] / cell_count - mean * mean + eps_norm)
    mean = jnp.repeat(mean, per_group)
    scale = jnp.repeat(scale, per_group)
    normed = (values - mean) * scale
    return jax.nn.silu(normed * gn_gain + gn_bias).astype(jnp.bfloat16)


def join_rims(parts, block_dim, dim, unit):
    size = parts.shape[dim]
    blocks = parts.shape[block_dim]
    core = lax.slice_in_dim(parts, unit, size - unit, axis=dim)
    low = lax.slice_in_dim(parts, 0, unit, axis=dim)
    high = lax.slice_in_dim(parts, size - unit, size, axis=dim)
    low = lax.slice_in_dim(low, 1, blocks, axis=block_dim)
    high = lax.slice_in_dim(high, 0, blocks - 1, axis=block_dim)
    pad_low = [(0, 0)] * parts.ndim
    pad_low[block_dim] = (0, 1)
    pad_low[dim] = (size - 3 * unit, 0)
    pad_high = [(0, 0)] * parts.ndim
    pad_high[block_dim] = (1, 0)
    pad_high[dim] = (0, size - 3 * unit)
    return core + jnp.pad(low, pad_low) + jnp.pad(high, pad_high)


def all_patches(activated, conv_weight, conv_bias):
    seq_n, head_n = (lax.axis_size("seq"), lax.axis_size("head"))
    frame_count, row_count, col_count, _ = activated.shape
    chans = conv_weight.shape[3]
    padded = jnp.concatenate([activated[:1], activated[:1], activated], axis=0)
    shares = lax.conv_general_dilated(
        padded[None],
        conv_weight,
        (1, 1, 1),
        ((0, 0), (2, 2), (2, 2)),
        dimension_numbers=("NDHWC", "DHWOI", "NDHWC"),
        preferred_element_type=jnp.float32,
    )[0]
    flat = shares.reshape(-1, 128)
    parts = lax.all_gather(flat, ("seq", "head"), axis=0, tiled=False)
    parts = parts.reshape(seq_n, head_n, frame_count, row_count + 2, (col_count + 2) * chans)
    parts = join_rims(join_rims(parts, 0, 3, 1), 1, 4, chans)
    latent = (parts + jnp.tile(conv_bias, col_count)).astype(jnp.bfloat16)
    blocks = latent.reshape(
        seq_n, head_n, frame_count, row_count // 2, 2, col_count // 2, 2 * chans
    )
    blocks = blocks.transpose(0, 1, 2, 3, 5, 4, 6)
    own = frame_count * (row_count // 2) * (col_count // 2)
    return blocks.reshape(seq_n * head_n * own, 4 * chans)


def modulate(patches, patch_weight, patch_bias, image_mod):
    hidden = jnp.dot(patches, patch_weight, preferred_element_type=jnp.float32) + patch_bias
    center = jnp.mean(hidden, axis=1, keepdims=True)
    offset = hidden - center
    spread = jnp.mean(offset * offset, axis=1, keepdims=True)
    normed = offset * lax.rsqrt(spread + eps_norm)
    return (normed * (1.0 + image_mod[1]) + image_mod[0]).astype(jnp.bfloat16)


def body(
    features,
    gn_gain,
    gn_bias,
    conv_weight,
    conv_bias,
    patch_weight,
    patch_bias,
    image_mod,
    w_qkv,
    text_ids,
    text_length,
    text_table,
    text_mod,
    w_text,
    w_out,
    out_bias,
):
    frame_count, row_count, col_count, _ = features.shape
    width_full = patch_weight.shape[1]
    seq_n, head_n = (lax.axis_size("seq"), lax.axis_size("head"))
    seq_i, head_i = (lax.axis_index("seq"), lax.axis_index("head"))
    depth, _, head_width = w_qkv.shape
    heads_here = head_width // HD
    group = seq_n // heads_here
    cols = head_width // seq_n
    text_count = text_ids.shape[0]
    both = jnp.concatenate([w_qkv, w_text], axis=1).reshape(depth, 5, seq_n, cols)
    both = both.transpose(2, 0, 1, 3).reshape(seq_n, depth, 5 * cols)
    both = lax.all_to_all(both, "seq", split_axis=0, concat_axis=0, tiled=True)
    both = both.reshape(seq_n * depth, 5, cols)
    both = group_gather(both, group, 2)
    w_query, w_image, w_text_full = (both[:, 0], both[:, 1:3], both[:, 3:5])
    chosen = (
        lax.broadcasted_iota(jnp.int32, (text_table.shape[1], text_count), 0) == text_ids[None, :]
    ).astype(jnp.bfloat16)
    own_context = jnp.dot(text_table, chosen, preferred_element_type=jnp.float32).astype(
        jnp.bfloat16
    )
    context = lax.all_gather(own_context, "seq", axis=0, tiled=True).astype(jnp.float32)
    mod = lax.all_gather(text_mod, "seq", axis=1, tiled=True)
    text_mean = jnp.sum(context, axis=0) / width_full
    text_square = jnp.sum(context * context, axis=0) / width_full
    text_scale = lax.rsqrt(text_square - text_mean * text_mean + eps_norm)
    text_normed = (context - text_mean) * text_scale * (1.0 + mod[1][:, None]) + mod[0][:, None]
    text_high = text_normed.astype(jnp.bfloat16)
    text_low = (text_normed - text_high.astype(jnp.float32)).astype(jnp.bfloat16)
    w_text_flat = w_text_full.reshape(width_full, 2 * HD)
    text_kv = sum(
        (
            lax.dot_general(
                part, w_text_flat, (((0,), (0,)), ((), ())), preferred_element_type=jnp.float32
            )
            for part in (text_high, text_low)
        )
    ).astype(jnp.bfloat16)
    activated = group_norm(features, gn_gain, gn_bias)
    patches = all_patches(activated, conv_weight, conv_bias)
    own = patches.shape[0] // (seq_n * head_n)
    part_rows = head_n * own // group
    my_part = seq_i % group
    chunk = min(CHUNK, patches.shape[0])

    def project(rows):
        modulated = modulate(rows, patch_weight, patch_bias, image_mod)
        kv = jnp.dot(
            modulated, w_image.reshape(width_full, 2 * HD), preferred_element_type=jnp.float32
        )
        query = jnp.dot(modulated, w_query, preferred_element_type=jnp.float32)
        query = lax.dynamic_index_in_dim(
            query.reshape(-1, group, part_rows, HD), my_part, axis=1, keepdims=False
        )
        return (kv.astype(jnp.bfloat16), query.reshape(-1, HD).astype(jnp.bfloat16))

    if chunk == patches.shape[0]:
        image_kv, query = project(patches)
    else:
        image_kv, query = lax.map(project, patches.reshape(-1, chunk, patches.shape[1]))
        image_kv = image_kv.reshape(-1, 2 * HD)
        query = query.reshape(-1, HD)
    keys = jnp.concatenate([image_kv[:, :HD], text_kv[:, :HD]], axis=0)
    vals = jnp.concatenate([image_kv[:, HD:], text_kv[:, HD:]], axis=0)
    key_valid = jnp.arange(keys.shape[0], dtype=jnp.int32) < image_kv.shape[0] + text_length[0]
    scores = (
        lax.dot_general(query, keys, (((1,), (1,)), ((), ())), preferred_element_type=jnp.float32)
        / HD
    )
    scores = jnp.where(key_valid[None, :], scores, -1e30)
    probs = jnp.exp(scores - jnp.max(scores, axis=1, keepdims=True))
    totals = jnp.sum(probs, axis=1, keepdims=True)
    attended = (
        jnp.dot(probs.astype(jnp.bfloat16), vals, preferred_element_type=jnp.float32) / totals
    ).astype(jnp.bfloat16)
    attended = attended.reshape(seq_n, part_rows, HD)
    attended = lax.all_to_all(attended, "seq", split_axis=0, concat_axis=0, tiled=True)
    attended = attended.reshape(heads_here, group, part_rows, HD).transpose(1, 2, 0, 3)
    attended = attended.reshape(head_n * own, head_width)
    if head_n == 2:
        halves = attended.reshape(2, own, head_width)
        away = jnp.dot(
            lax.dynamic_index_in_dim(halves, 1 - head_i, 0, keepdims=False),
            w_out,
            preferred_element_type=jnp.float32,
        )
        here = jnp.dot(
            lax.dynamic_index_in_dim(halves, head_i, 0, keepdims=False),
            w_out,
            preferred_element_type=jnp.float32,
        )
        projected = here + lax.ppermute(away, "head", [(0, 1), (1, 0)]) + out_bias
    else:
        projected = (
            lax.psum_scatter(
                jnp.dot(attended, w_out, preferred_element_type=jnp.float32),
                "head",
                scatter_dimension=0,
                tiled=True,
            )
            + out_bias
        )
    own_patches = lax.dynamic_slice_in_dim(patches, (seq_i * head_n + head_i) * own, own, axis=0)
    hidden = jnp.dot(own_patches, patch_weight, preferred_element_type=jnp.float32) + patch_bias
    block_out = (hidden + image_mod[2] * projected).astype(jnp.bfloat16)
    return block_out.reshape(frame_count, row_count // 2, col_count // 2, width_full)


def solution(mesh):
    return jax.shard_map(
        body,
        mesh=mesh,
        in_specs=(
            P(None, "seq", "head", None),
            P(),
            P(),
            P(),
            P(),
            P(),
            P(),
            P(),
            P("seq", None, "head"),
            P(),
            P(),
            P("seq", None),
            P(None, "seq"),
            P("seq", None, "head"),
            P("head", None),
            P(),
        ),
        out_specs=P(None, "seq", "head", None),
        check_vma=False,
    )
```

profile of v0, /device:TPU:0, one launch (start us, length us, event | category | flops | bytes accessed | tf_op | source)
XLA Modules:
  0.0 296.0 jit_solution(9451545067675089896)
XLA Ops:
  6.5 2.5 copy.83
  9.0 1.6 copy.82
  10.7 0.4 pad_maximum_fusion
  11.1 0.2 copy.84
  11.3 2.6 copy.85
  13.9 7.4 %all-to-all-start = ((bf16[16,192,320]{2,1,0:T(8,128)(2,1)}), bf16[16,192,320]{2,1,0:T(8,128)(2,1)}, u32[]{:S(2)}, u32[]{:S(2)}) async-start(bf16[16,192,320]{2,1,0:T(8,128)(2,1)} %copy.85), calls=%async_computation | async-start | bytes 4718592 | tf_op jit(solution)/shard_map/all_to_all | solution.py:132
  21.5 9.1 %fusion.23 = bf16[192,512]{1,0:T(8,128)(2,1)} fusion(bf16[192,16384]{1,0:T(8,128)(2,1)} %param.27, s32[512]{0:T(512)S(1)} %copy-done.19), kind=kOutput, calls=%fused_computation.34 | convolution fusion | flops 3229712384 | bytes 6490112 | tf_op jit(solution)/shard_map/dot_general | solution.py:139
  31.0 83.9 %psum.7 = f32[2,32]{1,0:T(2,128)S(1)} all-reduce(f32[2,32]{1,0:T(2,128)S(1)} %maximum_reduce_fusion), channel_id=1, replica_groups=mesh['seq'=16,'head'=2] {'seq','head'}, use_global_device_ids=true, to_apply=%region_3.4 | all-reduce | flops 64 | bytes 512 | tf_op jit(solution)/shard_map/psum | solution.py:34
  115.2 0.1 fusion.50
  115.4 4.2 %convolution_reduce_fusion = f32[8,4,6,16]{3,2,1,0:T(8,128)S(1)} fusion(bf16[3,3,3,16,512]{4,3,2,1,0:T(8,128)(2,1)S(1)} %copy-done, bf16[1,10,2,4,512]{4,3,2,1,0:T(4,128)(2,1)S(1)} %maximum_bitcast_fusion.2), kind=kOutput, calls=%fused_computation.36 | convolution fusion | flops 28311552 | bytes 536576 | tf_op jit(solution)/shard_map/conv_general_dilated | solution.py:73
  119.7 68.1 %all_gather.9 = f32[32,24,128]{2,1,0:T(8,128)S(1)} all-gather(f32[1,24,128]{2,1,0:T(8,128)S(1)} %all_gather_reshape_squeeze.3), channel_id=1, replica_groups=mesh['seq'=16,'head'=2] {'seq','head'}, dimensions={0}, use_global_device_ids=true | all-gather | bytes 405504 | tf_op jit(solution)/shard_map/all_gather | solution.py:82
  187.9 0.3 reshape.98
  188.2 0.1 slice.94
  188.4 0.2 fusion.65
  188.8 0.2 fusion.34
  189.0 0.1 reshape.99
  189.1 0.3 copy.81
  189.4 0.1 reshape.100
  189.6 3.6 %add_reduce_fusion = (f32[512]{0:T(512)S(1)}, f32[512,3072]{1,0:T(8,128)}) fusion(f32[3072]{0:T(1024)S(1)} %copy-done.11, bf16[512,64]{1,0:T(8,128)(2,1)S(1)} %reshape.100, bf16[64,3072]{1,0:T(8,128)(2,1)S(1)} %copy-done.7), kind=kOutput, calls=%fused_computation.15 | convolution fusion | flops 204471808 | bytes 6764544 | tf_op jit(solution)/shard_map/dot_general | solution.py:95
  193.2 17.4 %all-gather = f32[16,192,2]{1,2,0:T(2,128)S(1)} all-gather(f32[1,192,2]{1,2,0:T(2,128)S(1)} %bitcast.101), channel_id=1, replica_groups=mesh['seq'=16,'head'=2] {'seq'}, dimensions={0}, use_global_device_ids=true | all-gather | bytes 26112 | tf_op jit(solution)/shard_map/all_gather | solution.py:143
  210.8 3.9 %copy.86 = bf16[16,192,320]{1,0,2:T(8,128)(2,1)S(1)} copy(bf16[16,192,320]{2,1,0:T(8,128)(2,1)} %all-to-all-done) | data formatting | bytes 3932160 | tf_op jit(solution)/shard_map/all_to_all | solution.py:132
  214.7 3.7 %reshape.103 = bf16[3072,5,64]{0,2,1:T(8,128)(2,1)} reshape(bf16[16,192,320]{1,0,2:T(8,128)(2,1)S(1)} %copy.86) | data formatting | bytes 3932160 | tf_op jit(solution)/shard_map/reshape | solution.py:133
  218.4 0.3 collective-permute-start
  218.7 3.7 %multiply_reduce_fusion = f32[512]{0:T(512)S(1)} fusion(f32[512,3072]{1,0:T(8,128)} %get-tuple-element.29, f32[512]{0:T(512)S(1)} %broadcast_multiply_fusion.1, f32[3072]{0:T(1024)S(1)} %copy-done.11), kind=kLoop, calls=%fused_computation.14 | loop fusion | flops 6290944 | bytes 6307840 | tf_op jit(solution)/shard_map/reduce_sum | solution.py:98
  223.2 6.3 %add_convert_fusion = bf16[512,3072]{1,0:T(8,128)(2,1)} fusion(f32[512,3072]{1,0:T(8,128)} %get-tuple-element.29, f32[3072]{0:T(1024)S(1)} %bitcast.95, f32[3072]{0:T(1024)S(1)} %bitcast.96, f32[512]{0:T(512)S(1)} %add_rsqrt_fusion.1, f32[512]{0:T(512)S(1)} %broadcast_multiply_fusion.1, f32[3072]{0:T(1024)S(1)} %copy-done.11), kind=kLoop, calls=%fused_computation.13 | loop fusion | flops 9437184 | bytes 9478144 | tf_op jit(solution)/shard_map/convert_element_type | solution.py:100
  229.5 3.1 %copy.87 = bf16[3072,5,64]{2,0,1:T(8,128)(2,1)} copy(bf16[3072,5,64]{0,2,1:T(8,128)(2,1)S(1)} %copy-done.5) | data formatting | bytes 3932160 | tf_op jit(solution)/shard_map/reshape | solution.py:133
  232.6 4.7 %copy.88 = bf16[3072,5,64]{2,0,1:T(8,128)(2,1)} copy(bf16[3072,5,64]{0,2,1:T(8,128)(2,1)} %collective-permute-done) | data formatting | bytes 3932160 | tf_op jit(solution)/shard_map/ppermute | solution.py:17
  237.3 3.6 %broadcast_select_fusion.1 = (bf16[3072,5,64]{2,0,1:T(8,128)(2,1)S(1)}, bf16[3072,5,64]{2,0,1:T(8,128)(2,1)S(1)}) fusion(bf16[3072,5,64]{2,0,1:T(8,128)(2,1)} %copy.87, bf16[3072,5,64]{2,0,1:T(8,128)(2,1)} %copy.88, pred[]{:T(512)S(6)} %eq.14), kind=kLoop, calls=%fused_computation.17 | loop fusion | flops 1966080 | bytes 7864321 | tf_op jit(solution)/shard_map/jit(_where)/select_n | solution.py:20
  240.9 3.3 %pad_maximum_fusion.2 = (bf16[3072,2,128]{2,0,1:T(8,128)(2,1)S(1)}, bf16[3072,2,128]{2,0,1:T(8,128)(2,1)}) fusion(bf16[3072,5,64]{2,0,1:T(8,128)(2,1)S(1)} %get-tuple-element.12, bf16[3072,5,64]{2,0,1:T(8,128)(2,1)S(1)} %get-tuple-element.11), kind=kLoop, calls=%fused_computation.27 | loop fusion | flops 6291456 | bytes 7077888 | tf_op jit(solution)/shard_map/slice | solution.py:135
  244.3 0.2 copy-done.3
  244.4 2.6 copy.93
  247.0 1.6 copy.91
  248.6 3.5 %fusion.27 = bf16[16,2,16,128]{3,2,1,0:T(8,128)(2,1)S(1)} fusion(bf16[16,2,16,3072]{3,2,1,0:T(8,128)(2,1)} %bitcast.80, bf16[3072,5,64]{2,0,1:T(8,128)(2,1)} %copy-done.3, bf16[3072,5,64]{2,0,1:T(8,128)(2,1)} %copy-done.2), kind=kOutput, calls=%fused_computation.42 | convolution fusion | flops 404226048 | bytes 7208960 | tf_op jit(solution)/shard_map/dot_general | solution.py:171
  252.2 0.2 copy-done.9
  252.4 1.0 convolution_convert_fusion
  253.5 2.8 convert_reduce_fusion
  256.2 4.0 %fusion.43 = f32[512,256]{1,0:T(8,128)S(1)} fusion(bf16[3072,256]{0,1:T(8,128)(2,1)S(1)} %bitcast.83, bf16[3072,512]{1,0:T(8,128)(2,1)} %all-gather.3.cloned.1.call-done, f32[3072]{0:T(1024)S(1)} %bitcast.99, f32[3072]{0:T(1024)S(1)} %bitcast.97, f32[512]{0:T(512)S(1)} %get-tuple-element.27, f32[512]{0:T(512)S(1)} %get-tuple-element.26), kind=kOutput, calls=%fused_computation.58 | convolution fusion | flops 814743552 | bytes 5271552 | tf_op jit(solution)/shard_map/dot_general | solution.py:153
  260.3 2.1 fusion.19
  262.4 0.4 fusion.70
  262.8 0.3 fusion.25
  263.1 1.0 fusion.24
  264.1 3.6 %all-to-all-start.1 = ((bf16[16,16,128]{2,1,0:T(8,128)(2,1)}), bf16[16,16,128]{2,1,0:T(8,128)(2,1)S(1)}, u32[]{:S(2)}, u32[]{:S(2)}) async-start(bf16[16,16,128]{2,1,0:T(8,128)(2,1)} %bitcast.24), calls=%async_computation.1 | async-start | bytes 131072 | tf_op jit(solution)/shard_map/all_to_all | solution.py:197
  267.7 6.8 %all-to-all-done.1 = bf16[16,16,128]{2,1,0:T(8,128)(2,1)S(1)} async-done(((bf16[16,16,128]{2,1,0:T(8,128)(2,1)}), bf16[16,16,128]{2,1,0:T(8,128)(2,1)S(1)}, u32[]{:S(2)}, u32[]{:S(2)}) %all-to-all-start.1) | async-done | bytes 65568 | tf_op jit(solution)/shard_map/all_to_all | solution.py:197
  274.6 3.8 %fusion.51 = f32[16,3072]{1,0:T(8,128)S(1)} fusion(bf16[1024,3072]{1,0:T(8,128)(2,1)} %param.30, bf16[2,16,1024]{2,1,0:T(8,128)(2,1)S(1)} %bitcast.89, s32[]{:T(128)S(6)} %select_n.47), kind=kOutput, calls=%fused_computation.73 | convolution fusion | flops 100663296 | bytes 6520836 | tf_op jit(solution)/shard_map/dot_general | solution.py:202
  278.4 0.9 convolution_add_fusion
  279.2 5.5 %collective-permute-done.1 = f32[16,3072]{1,0:T(8,128)S(1)} collective-permute-done((f32[16,3072]{1,0:T(8,128)S(1)}, f32[16,3072]{1,0:T(8,128)S(1)}, u32[]{:S(2)}, u32[]{:S(2)}) %collective-permute-start.1) | collective-permute-done | bytes 196640 | tf_op jit(solution)/shard_map/ppermute | solution.py:212
  284.8 3.7 %fusion.12 = bf16[16,3072]{1,0:T(8,128)(2,1)S(1)} fusion(f32[16,3072]{1,0:T(8,128)S(1)} %convolution_add_fusion, f32[16,3072]{1,0:T(8,128)S(1)} %collective-permute-done.1, bf16[1024,3072]{1,0:T(8,128)(2,1)} %param.30, f32[3072]{0:T(1024)S(1)} %copy-done.14, f32[3072]{0:T(1024)S(1)} %bitcast.94, bf16[2,16,1024]{2,1,0:T(8,128)(2,1)S(1)} %bitcast.90, ...), kind=kOutput, calls=%fused_computation.23 | convolution fusion | flops 100909056 | bytes 6840324 | tf_op jit(solution)/shard_map/dot_general | solution.py:207
  288.5 0.7 reshape.108
  (73 shorter events, 1.4 us)
Async XLA Ops:
  6.5 108.8 %copy-start = (bf16[3,3,3,16,512]{4,3,2,1,0:T(8,128)(2,1)S(1)}, bf16[3,3,3,16,512]{4,3,2,1,0:T(8,128)(2,1)}, u32[]{:S(2)}) copy-start(bf16[3,3,3,16,512]{4,3,2,1,0:T(8,128)(2,1)} %param.19) | copy-start | bytes 1327108
  11.3 10.1 %copy-start.19 = (s32[512]{0:T(512)S(1)}, s32[512]{0:T(512)}, u32[]{:S(2)}) copy-start(s32[512]{0:T(512)} %param.25) | copy-start | bytes 6148
  13.9 196.8 %all-to-all-start = ((bf16[16,192,320]{2,1,0:T(8,128)(2,1)}), bf16[16,192,320]{2,1,0:T(8,128)(2,1)}, u32[]{:S(2)}, u32[]{:S(2)}) async-start(bf16[16,192,320]{2,1,0:T(8,128)(2,1)} %copy.85), calls=%async_computation | async-start | bytes 4718592 | tf_op jit(solution)/shard_map/all_to_all | solution.py:132
  21.4 9.3 %copy-start.12 = (bf16[8,2,4,512]{3,2,1,0:T(4,128)(2,1)S(1)}, bf16[8,2,4,512]{3,2,1,0:T(4,128)(2,1)}, u32[]{:S(2)}) copy-start(bf16[8,2,4,512]{3,2,1,0:T(4,128)(2,1)} %param.16) | copy-start | bytes 196612
  21.4 93.8 %copy-start.15 = (f32[512]{0:T(512)S(1)}, f32[512]{0:T(512)}, u32[]{:S(2)}) copy-start(f32[512]{0:T(512)} %param.18) | copy-start | bytes 6148
  21.4 93.8 %copy-start.16 = (f32[512]{0:T(512)S(1)}, f32[512]{0:T(512)}, u32[]{:S(2)}) copy-start(f32[512]{0:T(512)} %param.17) | copy-start | bytes 6148
  21.4 167.0 %copy-start.18 = (f32[16]{0:T(128)S(1)}, f32[16]{0:T(128)}, u32[]{:S(2)}) copy-start(f32[16]{0:T(128)} %param.20) | copy-start | bytes 196
  21.4 232.0 %all-gather.3.cloned.1.call-start = ((), (), s32[]{:S(2)}) async-start(), calls=%async_computation.2 | async-start | bytes 3342336 | tf_op jit(solution)/shard_map/all_gather | solution.py:142
  30.6 158.9 %copy-start.7 = (bf16[64,3072]{1,0:T(8,128)(2,1)S(1)}, bf16[64,3072]{1,0:T(8,128)(2,1)}, u32[]{:S(2)}) copy-start(bf16[64,3072]{1,0:T(8,128)(2,1)} %param.21) | copy-start | bytes 1179652
  30.6 158.9 %copy-start.11 = (f32[3072]{0:T(1024)S(1)}, f32[3072]{0:T(1024)}, u32[]{:S(2)}) copy-start(f32[3072]{0:T(1024)} %param.22) | copy-start | bytes 36868
  189.5 3.7 %copy-start.10 = (bf16[512,64]{1,0:T(8,128)(2,1)}, bf16[512,64]{1,0:T(8,128)(2,1)S(1)}, u32[]{:S(2)}) copy-start(bf16[512,64]{1,0:T(8,128)(2,1)S(1)} %reshape.100) | copy-start | bytes 196612
  189.6 3.6 %copy-start.17 = (f32[2,192]{1,0:T(2,128)S(1)}, f32[2,192]{1,0:T(2,128)}, u32[]{:S(2)}) copy-start(f32[2,192]{1,0:T(2,128)} %param.28) | copy-start | bytes 4612
  218.4 4.7 %copy-start.13 = (f32[3,3072]{1,0:T(4,128)S(1)}, f32[3,3072]{1,0:T(4,128)}, u32[]{:S(2)}) copy-start(f32[3,3072]{1,0:T(4,128)} %param.23) | copy-start | bytes 110596
  218.4 14.2 %collective-permute-start = (bf16[3072,5,64]{0,2,1:T(8,128)(2,1)}, bf16[3072,5,64]{0,2,1:T(8,128)(2,1)}, u32[]{:S(2)}, u32[]{:S(2)}) collective-permute-start(bf16[3072,5,64]{0,2,1:T(8,128)(2,1)} %reshape.103), channel_id=1, source_target_pairs={{0,2},{2,0},{4,6},{6,4},{8,10},{10,8},{12,14},{14,12},{16,18},{18,... | collective-permute-start | bytes 5898248 | tf_op jit(solution)/shard_map/ppermute | solution.py:17
  223.2 6.3 %copy-start.5 = (bf16[3072,5,64]{0,2,1:T(8,128)(2,1)S(1)}, bf16[3072,5,64]{0,2,1:T(8,128)(2,1)}, u32[]{:S(2)}) copy-start(bf16[3072,5,64]{0,2,1:T(8,128)(2,1)} %reshape.103) | copy-start | bytes 5898244
  240.9 3.4 %copy-start.2 = (bf16[3072,5,64]{2,0,1:T(8,128)(2,1)}, bf16[3072,5,64]{2,0,1:T(8,128)(2,1)S(1)}, u32[]{:S(2)}) copy-start(bf16[3072,5,64]{2,0,1:T(8,128)(2,1)S(1)} %get-tuple-element.11) | copy-start | bytes 5898244
  240.9 3.5 %copy-start.3 = (bf16[3072,5,64]{2,0,1:T(8,128)(2,1)}, bf16[3072,5,64]{2,0,1:T(8,128)(2,1)S(1)}, u32[]{:S(2)}) copy-start(bf16[3072,5,64]{2,0,1:T(8,128)(2,1)S(1)} %get-tuple-element.12) | copy-start | bytes 5898244
  248.6 3.6 %copy-start.4 = (bf16[512,3072]{1,0:T(8,128)(2,1)S(1)}, bf16[512,3072]{1,0:T(8,128)(2,1)}, u32[]{:S(2)}) copy-start(bf16[512,3072]{1,0:T(8,128)(2,1)} %add_convert_fusion) | copy-start | bytes 9437188
  248.6 3.8 %copy-start.9 = (bf16[3072,2,128]{0,2,1:T(8,128)(2,1)S(1)}, bf16[3072,2,128]{0,2,1:T(8,128)(2,1)}, u32[]{:S(2)}) copy-start(bf16[3072,2,128]{0,2,1:T(8,128)(2,1)} %copy.91) | copy-start | bytes 4718596
  252.4 3.9 %copy-start.8 = (bf16[3072,2,128]{0,2,1:T(8,128)(2,1)S(1)}, bf16[3072,2,128]{0,2,1:T(8,128)(2,1)}, u32[]{:S(2)}) copy-start(bf16[3072,2,128]{0,2,1:T(8,128)(2,1)} %copy.93) | copy-start | bytes 4718596
  256.2 4.0 %copy-start.6 = (bf16[3072,512]{1,0:T(8,128)(2,1)S(1)}, bf16[3072,512]{1,0:T(8,128)(2,1)}, u32[]{:S(2)}) copy-start(bf16[3072,512]{1,0:T(8,128)(2,1)} %all-gather.3.cloned.1.call-done) | copy-start | bytes 9437188
  264.1 20.7 %copy-start.14 = (f32[3072]{0:T(1024)S(1)}, f32[3072]{0:T(1024)}, u32[]{:S(2)}) copy-start(f32[3072]{0:T(1024)} %param.31) | copy-start | bytes 36868
  264.1 10.5 %all-to-all-start.1 = ((bf16[16,16,128]{2,1,0:T(8,128)(2,1)}), bf16[16,16,128]{2,1,0:T(8,128)(2,1)S(1)}, u32[]{:S(2)}, u32[]{:S(2)}) async-start(bf16[16,16,128]{2,1,0:T(8,128)(2,1)} %bitcast.24), calls=%async_computation.1 | async-start | bytes 131072 | tf_op jit(solution)/shard_map/all_to_all | solution.py:197
  274.6 14.6 %copy-start.1 = (bf16[3,3,3,16,512]{4,3,2,1,0:T(8,128)(2,1)S(1)}, bf16[3,3,3,16,512]{4,3,2,1,0:T(8,128)(2,1)}, u32[]{:S(2)}) copy-start(bf16[3,3,3,16,512]{4,3,2,1,0:T(8,128)(2,1)} %param.19) | copy-start | bytes 1327108
  278.4 6.4 %collective-permute-start.1 = (f32[16,3072]{1,0:T(8,128)S(1)}, f32[16,3072]{1,0:T(8,128)S(1)}, u32[]{:S(2)}, u32[]{:S(2)}) collective-permute-start(f32[16,3072]{1,0:T(8,128)S(1)} %fusion.51), channel_id=1, source_target_pairs={{0,1},{1,0},{2,3},{3,2},{4,5},{5,4},{6,7},{7,6},{8,9},{9,8},{10,11... | collective-permute-start | bytes 589832 | tf_op jit(solution)/shard_map/ppermute | solution.py:212
Sparse Core Ops, SparseCore 0:
  30.8 66.3 all-gather.2
where the time goes:
time: 297 us; the launch traced here: 296 us
  blocking collectives  169 us (57%)
  matrix products  37.4 us (13%)
  local copies, waits for them, and re-layouts  29.8 us (10%)
  other arithmetic  21.1 us (7%)
  between operations  14.6 us (5%)
  waiting for transfers between devices  12.4 us (4%)
  starting transfers between devices  11.4 us (4%)
    psum x1, blocking collectives, group_norm(): sums = lax.psum(sums, ('seq', 'head'))  83.9 us
    all_gather x1, blocking collectives, all_patches(): parts = lax.all_gather(flat, ('seq', 'head'), axis=0, tiled=False)  68.1 us
    all_gather x1, blocking collectives, body(): mod = lax.all_gather(text_mod, 'seq', axis=1, tiled=True)  17.4 us
    dot_general x1, matrix products, body(): jnp.dot(text_table, chosen, preferred_element_type=jnp.float32)  9.15 us
    all_to_all x1, starting transfers between devices, body(): both = lax.all_to_all(both, 'seq', split_axis=0, concat_axis=0, tiled=True)  7.4 us
    all_to_all x1, waiting for transfers between devices, body(): lax.all_to_all(attended, 'seq', split_axis=0, concat_axis=0, tiled=True)  6.85 us
    reshape x2, local copies, waits for them, and re-layouts, body(): both = both.reshape(seq_n * depth, 5, cols)  6.84 us
    convert_element_type x1, other arithmetic, modulate(): return (normed * (1.0 + image_mod[1]) + image_mod[0]).astype(jnp.bfloat16)  6.3 us
  transfers between devices with their start and end apart: 5, of which 2 were waited for; matrix products, arithmetic and copies ran while one was open for 21% of the time, Pallas kernels for 0%

commit v1 on v0

--- a/solution.py
+++ b/solution.py
@@ -31,7 +31,7 @@
         [jnp.sum(values, axis=(0, 1, 2)), jnp.sum(values * values, axis=(0, 1, 2))]
     )
     sums = jnp.sum(chan_sums.reshape(2, GN_GROUPS, per_group), axis=2)
-    sums = lax.psum(sums, ("seq", "head"))
+    sums = jnp.sum(lax.all_gather(sums, ("seq", "head")), axis=0)
     cell_count = (
         frame_count
         * row_count

time: 297 us -> 310 us (1.044)
  blocking collectives: 169 us -> 183 us
    all_gather x0 -> x1, blocking collectives: none -> 97.5 us  [group_norm(): sums = jnp.sum(lax.all_gather(sums, ('seq', 'head')), axis=0)]
    psum x1 -> x0, blocking collectives: 83.9 us -> none  [group_norm(): sums = lax.psum(sums, ('seq', 'head'))]
  transfers between devices with their start and end apart: 5 -> 5, of which waited for: 2 -> 2; matrix products, arithmetic and copies ran while one was open for 21% -> 20% of each run, Pallas kernels for 0% -> 0%
where the time goes in v1:
time: 310 us; the launch traced here: 309 us
  blocking collectives  183 us (59%)
  matrix products  37.4 us (12%)
  local copies, waits for them, and re-layouts  29.8 us (10%)
  other arithmetic  21.1 us (7%)
  between operations  14.6 us (5%)
  waiting for transfers between devices  12.4 us (4%)
  starting transfers between devices  11.4 us (4%)
    all_gather x1, blocking collectives, group_norm(): sums = jnp.sum(lax.all_gather(sums, ('seq', 'head')), axis=0)  97.5 us
    all_gather x1, blocking collectives, all_patches(): parts = lax.all_gather(flat, ('seq', 'head'), axis=0, tiled=False)  67.9 us
    all_gather x1, blocking collectives, body(): mod = lax.all_gather(text_mod, 'seq', axis=1, tiled=True)  17.4 us
    dot_general x1, matrix products, body(): jnp.dot(text_table, chosen, preferred_element_type=jnp.float32)  9.15 us
    all_to_all x1, starting transfers between devices, body(): both = lax.all_to_all(both, 'seq', split_axis=0, concat_axis=0, tiled=True)  7.4 us
    all_to_all x1, waiting for transfers between devices, body(): lax.all_to_all(attended, 'seq', split_axis=0, concat_axis=0, tiled=True)  6.85 us
    reshape x2, local copies, waits for them, and re-layouts, body(): both = both.reshape(seq_n * depth, 5, cols)  6.84 us
    convert_element_type x1, other arithmetic, modulate(): return (normed * (1.0 + image_mod[1]) + image_mod[0]).astype(jnp.bfloat16)  6.3 us
  transfers between devices with their start and end apart: 5, of which 2 were waited for; matrix products, arithmetic and copies ran while one was open for 20% of the time, Pallas kernels for 0%

profile of v1, /device:TPU:0, one launch (start us, length us, event | category | flops | bytes accessed | tf_op | source)
XLA Modules:
  0.0 309.5 jit_solution(18129063665708863828)
XLA Ops:
  6.5 2.5 copy.83
  9.0 1.6 copy.82
  10.7 0.4 pad_maximum_fusion
  11.1 0.2 copy.84
  11.3 2.6 copy.85
  13.9 7.4 %all-to-all-start = ((bf16[16,192,320]{2,1,0:T(8,128)(2,1)}), bf16[16,192,320]{2,1,0:T(8,128)(2,1)}, u32[]{:S(2)}, u32[]{:S(2)}) async-start(bf16[16,192,320]{2,1,0:T(8,128)(2,1)} %copy.85), calls=%async_computation | async-start | bytes 4718592 | tf_op jit(solution)/shard_map/all_to_all | solution.py:132
  21.5 9.1 %fusion.23 = bf16[192,512]{1,0:T(8,128)(2,1)} fusion(bf16[192,16384]{1,0:T(8,128)(2,1)} %param.27, s32[512]{0:T(512)S(1)} %copy-done.19), kind=kOutput, calls=%fused_computation.34 | convolution fusion | flops 3229712384 | bytes 6490112 | tf_op jit(solution)/shard_map/dot_general | solution.py:139
  31.0 97.5 %all-gather.1 = f32[32,2,32]{2,1,0:T(2,128)S(1)} all-gather(f32[1,2,32]{2,1,0:T(2,128)S(1)} %bitcast.102), channel_id=2, replica_groups=mesh['seq'=16,'head'=2] {'seq','head'}, dimensions={0}, use_global_device_ids=true | all-gather | bytes 8448 | tf_op jit(solution)/shard_map/all_gather | solution.py:34
  128.9 0.1 fusion.50
  129.1 4.2 %convolution_reduce_fusion = f32[8,4,6,16]{3,2,1,0:T(8,128)S(1)} fusion(bf16[3,3,3,16,512]{4,3,2,1,0:T(8,128)(2,1)S(1)} %copy-done, bf16[1,10,2,4,512]{4,3,2,1,0:T(4,128)(2,1)S(1)} %maximum_bitcast_fusion.2), kind=kOutput, calls=%fused_computation.36 | convolution fusion | flops 28311552 | bytes 536576 | tf_op jit(solution)/shard_map/conv_general_dilated | solution.py:73
  133.4 67.9 %all_gather.17 = f32[32,24,128]{2,1,0:T(8,128)S(1)} all-gather(f32[1,24,128]{2,1,0:T(8,128)S(1)} %all_gather_reshape_squeeze.3), channel_id=1, replica_groups=mesh['seq'=16,'head'=2] {'seq','head'}, dimensions={0}, use_global_device_ids=true | all-gather | bytes 405504 | tf_op jit(solution)/shard_map/all_gather | solution.py:82
  201.3 0.3 reshape.98
  201.6 0.1 slice.94
  201.9 0.2 fusion.65
  202.2 0.2 fusion.34
  202.4 0.1 reshape.99
  202.5 0.3 copy.81
  202.8 0.1 reshape.100
  203.0 3.6 %add_reduce_fusion = (f32[512]{0:T(512)S(1)}, f32[512,3072]{1,0:T(8,128)}) fusion(f32[3072]{0:T(1024)S(1)} %copy-done.11, bf16[512,64]{1,0:T(8,128)(2,1)S(1)} %reshape.100, bf16[64,3072]{1,0:T(8,128)(2,1)S(1)} %copy-done.7), kind=kOutput, calls=%fused_computation.15 | convolution fusion | flops 204471808 | bytes 6764544 | tf_op jit(solution)/shard_map/dot_general | solution.py:95
  206.6 17.4 %all-gather.2 = f32[16,192,2]{1,2,0:T(2,128)S(1)} all-gather(f32[1,192,2]{1,2,0:T(2,128)S(1)} %bitcast.103), channel_id=1, replica_groups=mesh['seq'=16,'head'=2] {'seq'}, dimensions={0}, use_global_device_ids=true | all-gather | bytes 26112 | tf_op jit(solution)/shard_map/all_gather | solution.py:143
  224.2 3.9 %copy.86 = bf16[16,192,320]{1,0,2:T(8,128)(2,1)S(1)} copy(bf16[16,192,320]{2,1,0:T(8,128)(2,1)} %all-to-all-done) | data formatting | bytes 3932160 | tf_op jit(solution)/shard_map/all_to_all | solution.py:132
  228.1 3.7 %reshape.103 = bf16[3072,5,64]{0,2,1:T(8,128)(2,1)} reshape(bf16[16,192,320]{1,0,2:T(8,128)(2,1)S(1)} %copy.86) | data formatting | bytes 3932160 | tf_op jit(solution)/shard_map/reshape | solution.py:133
  231.8 0.3 collective-permute-start
  232.2 3.7 %multiply_reduce_fusion = f32[512]{0:T(512)S(1)} fusion(f32[512,3072]{1,0:T(8,128)} %get-tuple-element.29, f32[512]{0:T(512)S(1)} %broadcast_multiply_fusion.1, f32[3072]{0:T(1024)S(1)} %copy-done.11), kind=kLoop, calls=%fused_computation.14 | loop fusion | flops 6290944 | bytes 6307840 | tf_op jit(solution)/shard_map/reduce_sum | solution.py:98
  236.6 6.3 %add_convert_fusion = bf16[512,3072]{1,0:T(8,128)(2,1)} fusion(f32[512,3072]{1,0:T(8,128)} %get-tuple-element.29, f32[3072]{0:T(1024)S(1)} %bitcast.96, f32[3072]{0:T(1024)S(1)} %bitcast.97, f32[512]{0:T(512)S(1)} %add_rsqrt_fusion.1, f32[512]{0:T(512)S(1)} %broadcast_multiply_fusion.1, f32[3072]{0:T(1024)S(1)} %copy-done.11), kind=kLoop, calls=%fused_computation.13 | loop fusion | flops 9437184 | bytes 9478144 | tf_op jit(solution)/shard_map/convert_element_type | solution.py:100
  242.9 3.1 copy.87
  246.0 4.7 %copy.88 = bf16[3072,5,64]{2,0,1:T(8,128)(2,1)} copy(bf16[3072,5,64]{0,2,1:T(8,128)(2,1)} %collective-permute-done) | data formatting | bytes 3932160 | tf_op jit(solution)/shard_map/ppermute | solution.py:17
  250.7 3.6 %broadcast_select_fusion.1 = (bf16[3072,5,64]{2,0,1:T(8,128)(2,1)S(1)}, bf16[3072,5,64]{2,0,1:T(8,128)(2,1)S(1)}) fusion(bf16[3072,5,64]{2,0,1:T(8,128)(2,1)} %copy.87, bf16[3072,5,64]{2,0,1:T(8,128)(2,1)} %copy.88, pred[]{:T(512)S(6)} %eq.14), kind=kLoop, calls=%fused_computation.17 | loop fusion | flops 1966080 | bytes 7864321 | tf_op jit(solution)/shard_map/jit(_where)/select_n | solution.py:20
  254.4 3.3 %pad_maximum_fusion.2 = (bf16[3072,2,128]{2,0,1:T(8,128)(2,1)S(1)}, bf16[3072,2,128]{2,0,1:T(8,128)(2,1)}) fusion(bf16[3072,5,64]{2,0,1:T(8,128)(2,1)S(1)} %get-tuple-element.12, bf16[3072,5,64]{2,0,1:T(8,128)(2,1)S(1)} %get-tuple-element.11), kind=kLoop, calls=%fused_computation.27 | loop fusion | flops 6291456 | bytes 7077888 | tf_op jit(solution)/shard_map/slice | solution.py:135
  257.7 0.2 copy-done.3
  257.9 2.6 copy.93
  260.5 1.6 copy.91
  262.0 3.5 %fusion.27 = bf16[16,2,16,128]{3,2,1,0:T(8,128)(2,1)S(1)} fusion(bf16[16,2,16,3072]{3,2,1,0:T(8,128)(2,1)} %bitcast.81, bf16[3072,5,64]{2,0,1:T(8,128)(2,1)} %copy-done.3, bf16[3072,5,64]{2,0,1:T(8,128)(2,1)} %copy-done.2), kind=kOutput, calls=%fused_computation.42 | convolution fusion | flops 404226048 | bytes 7208960 | tf_op jit(solution)/shard_map/dot_general | solution.py:171
  265.6 0.2 copy-done.9
  265.8 1.0 convolution_convert_fusion
  266.9 2.8 convert_reduce_fusion
  269.7 4.0 %fusion.43 = f32[512,256]{1,0:T(8,128)S(1)} fusion(bf16[3072,256]{0,1:T(8,128)(2,1)S(1)} %bitcast.84, bf16[3072,512]{1,0:T(8,128)(2,1)} %all-gather.5.cloned.1.call-done, f32[3072]{0:T(1024)S(1)} %bitcast.100, f32[3072]{0:T(1024)S(1)} %bitcast.98, f32[512]{0:T(512)S(1)} %get-tuple-element.27, f32[512]{0:T(512)S(1)} %get-tuple-element.26), kind=kOutput, calls=%fused_computation.58 | convolution fusion | flops 814743552 | bytes 5271552 | tf_op jit(solution)/shard_map/dot_general | solution.py:153
  273.7 2.1 fusion.19
  275.8 0.4 fusion.70
  276.2 0.3 fusion.25
  276.5 1.0 fusion.24
  277.5 3.6 %all-to-all-start.1 = ((bf16[16,16,128]{2,1,0:T(8,128)(2,1)}), bf16[16,16,128]{2,1,0:T(8,128)(2,1)S(1)}, u32[]{:S(2)}, u32[]{:S(2)}) async-start(bf16[16,16,128]{2,1,0:T(8,128)(2,1)} %bitcast.25), calls=%async_computation.1 | async-start | bytes 131072 | tf_op jit(solution)/shard_map/all_to_all | solution.py:197
  281.2 6.8 %all-to-all-done.1 = bf16[16,16,128]{2,1,0:T(8,128)(2,1)S(1)} async-done(((bf16[16,16,128]{2,1,0:T(8,128)(2,1)}), bf16[16,16,128]{2,1,0:T(8,128)(2,1)S(1)}, u32[]{:S(2)}, u32[]{:S(2)}) %all-to-all-start.1) | async-done | bytes 65568 | tf_op jit(solution)/shard_map/all_to_all | solution.py:197
  288.0 3.8 %fusion.51 = f32[16,3072]{1,0:T(8,128)S(1)} fusion(bf16[1024,3072]{1,0:T(8,128)(2,1)} %param.30, bf16[2,16,1024]{2,1,0:T(8,128)(2,1)S(1)} %bitcast.90, s32[]{:T(128)S(6)} %select_n.47), kind=kOutput, calls=%fused_computation.73 | convolution fusion | flops 100663296 | bytes 6520836 | tf_op jit(solution)/shard_map/dot_general | solution.py:202
  291.8 0.9 convolution_add_fusion
  292.7 5.5 %collective-permute-done.1 = f32[16,3072]{1,0:T(8,128)S(1)} collective-permute-done((f32[16,3072]{1,0:T(8,128)S(1)}, f32[16,3072]{1,0:T(8,128)S(1)}, u32[]{:S(2)}, u32[]{:S(2)}) %collective-permute-start.1) | collective-permute-done | bytes 196640 | tf_op jit(solution)/shard_map/ppermute | solution.py:212
  298.2 3.7 %fusion.12 = bf16[16,3072]{1,0:T(8,128)(2,1)S(1)} fusion(f32[16,3072]{1,0:T(8,128)S(1)} %convolution_add_fusion, f32[16,3072]{1,0:T(8,128)S(1)} %collective-permute-done.1, bf16[1024,3072]{1,0:T(8,128)(2,1)} %param.30, f32[3072]{0:T(1024)S(1)} %copy-done.14, f32[3072]{0:T(1024)S(1)} %bitcast.95, bf16[2,16,1024]{2,1,0:T(8,128)(2,1)S(1)} %bitcast.91, ...), kind=kOutput, calls=%fused_computation.23 | convolution fusion | flops 100909056 | bytes 6840324 | tf_op jit(solution)/shard_map/dot_general | solution.py:207
  301.9 0.7 reshape.108
  (74 shorter events, 1.5 us)
Async XLA Ops:
  6.5 122.5 %copy-start = (bf16[3,3,3,16,512]{4,3,2,1,0:T(8,128)(2,1)S(1)}, bf16[3,3,3,16,512]{4,3,2,1,0:T(8,128)(2,1)}, u32[]{:S(2)}) copy-start(bf16[3,3,3,16,512]{4,3,2,1,0:T(8,128)(2,1)} %param.19) | copy-start | bytes 1327108
  11.3 10.1 %copy-start.19 = (s32[512]{0:T(512)S(1)}, s32[512]{0:T(512)}, u32[]{:S(2)}) copy-start(s32[512]{0:T(512)} %param.25) | copy-start | bytes 6148
  13.9 210.2 %all-to-all-start = ((bf16[16,192,320]{2,1,0:T(8,128)(2,1)}), bf16[16,192,320]{2,1,0:T(8,128)(2,1)}, u32[]{:S(2)}, u32[]{:S(2)}) async-start(bf16[16,192,320]{2,1,0:T(8,128)(2,1)} %copy.85), calls=%async_computation | async-start | bytes 4718592 | tf_op jit(solution)/shard_map/all_to_all | solution.py:132
  21.4 9.3 %copy-start.12 = (bf16[8,2,4,512]{3,2,1,0:T(4,128)(2,1)S(1)}, bf16[8,2,4,512]{3,2,1,0:T(4,128)(2,1)}, u32[]{:S(2)}) copy-start(bf16[8,2,4,512]{3,2,1,0:T(4,128)(2,1)} %param.16) | copy-start | bytes 196612
  21.4 107.5 %copy-start.15 = (f32[512]{0:T(512)S(1)}, f32[512]{0:T(512)}, u32[]{:S(2)}) copy-start(f32[512]{0:T(512)} %param.18) | copy-start | bytes 6148
  21.4 107.5 %copy-start.16 = (f32[512]{0:T(512)S(1)}, f32[512]{0:T(512)}, u32[]{:S(2)}) copy-start(f32[512]{0:T(512)} %param.17) | copy-start | bytes 6148
  21.4 180.4 %copy-start.18 = (f32[16]{0:T(128)S(1)}, f32[16]{0:T(128)}, u32[]{:S(2)}) copy-start(f32[16]{0:T(128)} %param.20) | copy-start | bytes 196
  21.4 245.5 %all-gather.5.cloned.1.call-start = ((), (), s32[]{:S(2)}) async-start(), calls=%async_computation.2 | async-start | bytes 3342336 | tf_op jit(solution)/shard_map/all_gather | solution.py:142
  30.6 172.4 %copy-start.7 = (bf16[64,3072]{1,0:T(8,128)(2,1)S(1)}, bf16[64,3072]{1,0:T(8,128)(2,1)}, u32[]{:S(2)}) copy-start(bf16[64,3072]{1,0:T(8,128)(2,1)} %param.21) | copy-start | bytes 1179652
  30.6 172.4 %copy-start.11 = (f32[3072]{0:T(1024)S(1)}, f32[3072]{0:T(1024)}, u32[]{:S(2)}) copy-start(f32[3072]{0:T(1024)} %param.22) | copy-start | bytes 36868
  203.0 3.7 %copy-start.10 = (bf16[512,64]{1,0:T(8,128)(2,1)}, bf16[512,64]{1,0:T(8,128)(2,1)S(1)}, u32[]{:S(2)}) copy-start(bf16[512,64]{1,0:T(8,128)(2,1)S(1)} %reshape.100) | copy-start | bytes 196612
  203.0 3.6 %copy-start.17 = (f32[2,192]{1,0:T(2,128)S(1)}, f32[2,192]{1,0:T(2,128)}, u32[]{:S(2)}) copy-start(f32[2,192]{1,0:T(2,128)} %param.28) | copy-start | bytes 4612
  231.8 4.7 %copy-start.13 = (f32[3,3072]{1,0:T(4,128)S(1)}, f32[3,3072]{1,0:T(4,128)}, u32[]{:S(2)}) copy-start(f32[3,3072]{1,0:T(4,128)} %param.23) | copy-start | bytes 110596
  231.8 14.2 %collective-permute-start = (bf16[3072,5,64]{0,2,1:T(8,128)(2,1)}, bf16[3072,5,64]{0,2,1:T(8,128)(2,1)}, u32[]{:S(2)}, u32[]{:S(2)}) collective-permute-start(bf16[3072,5,64]{0,2,1:T(8,128)(2,1)} %reshape.103), channel_id=1, source_target_pairs={{0,2},{2,0},{4,6},{6,4},{8,10},{10,8},{12,14},{14,12},{16,18},{18,... | collective-permute-start | bytes 5898248 | tf_op jit(solution)/shard_map/ppermute | solution.py:17
  236.6 6.3 %copy-start.5 = (bf16[3072,5,64]{0,2,1:T(8,128)(2,1)S(1)}, bf16[3072,5,64]{0,2,1:T(8,128)(2,1)}, u32[]{:S(2)}) copy-start(bf16[3072,5,64]{0,2,1:T(8,128)(2,1)} %reshape.103) | copy-start | bytes 5898244
  254.3 3.4 %copy-start.2 = (bf16[3072,5,64]{2,0,1:T(8,128)(2,1)}, bf16[3072,5,64]{2,0,1:T(8,128)(2,1)S(1)}, u32[]{:S(2)}) copy-start(bf16[3072,5,64]{2,0,1:T(8,128)(2,1)S(1)} %get-tuple-element.11) | copy-start | bytes 5898244
  254.3 3.5 %copy-start.3 = (bf16[3072,5,64]{2,0,1:T(8,128)(2,1)}, bf16[3072,5,64]{2,0,1:T(8,128)(2,1)S(1)}, u32[]{:S(2)}) copy-start(bf16[3072,5,64]{2,0,1:T(8,128)(2,1)S(1)} %get-tuple-element.12) | copy-start | bytes 5898244
  262.0 3.6 %copy-start.4 = (bf16[512,3072]{1,0:T(8,128)(2,1)S(1)}, bf16[512,3072]{1,0:T(8,128)(2,1)}, u32[]{:S(2)}) copy-start(bf16[512,3072]{1,0:T(8,128)(2,1)} %add_convert_fusion) | copy-start | bytes 9437188
  262.0 3.8 %copy-start.9 = (bf16[3072,2,128]{0,2,1:T(8,128)(2,1)S(1)}, bf16[3072,2,128]{0,2,1:T(8,128)(2,1)}, u32[]{:S(2)}) copy-start(bf16[3072,2,128]{0,2,1:T(8,128)(2,1)} %copy.91) | copy-start | bytes 4718596
  265.8 3.9 %copy-start.8 = (bf16[3072,2,128]{0,2,1:T(8,128)(2,1)S(1)}, bf16[3072,2,128]{0,2,1:T(8,128)(2,1)}, u32[]{:S(2)}) copy-start(bf16[3072,2,128]{0,2,1:T(8,128)(2,1)} %copy.93) | copy-start | bytes 4718596
  269.7 4.0 %copy-start.6 = (bf16[3072,512]{1,0:T(8,128)(2,1)S(1)}, bf16[3072,512]{1,0:T(8,128)(2,1)}, u32[]{:S(2)}) copy-start(bf16[3072,512]{1,0:T(8,128)(2,1)} %all-gather.5.cloned.1.call-done) | copy-start | bytes 9437188
  277.5 20.7 %copy-start.14 = (f32[3072]{0:T(1024)S(1)}, f32[3072]{0:T(1024)}, u32[]{:S(2)}) copy-start(f32[3072]{0:T(1024)} %param.31) | copy-start | bytes 36868
  277.5 10.5 %all-to-all-start.1 = ((bf16[16,16,128]{2,1,0:T(8,128)(2,1)}), bf16[16,16,128]{2,1,0:T(8,128)(2,1)S(1)}, u32[]{:S(2)}, u32[]{:S(2)}) async-start(bf16[16,16,128]{2,1,0:T(8,128)(2,1)} %bitcast.25), calls=%async_computation.1 | async-start | bytes 131072 | tf_op jit(solution)/shard_map/all_to_all | solution.py:197
  288.0 14.6 %copy-start.1 = (bf16[3,3,3,16,512]{4,3,2,1,0:T(8,128)(2,1)S(1)}, bf16[3,3,3,16,512]{4,3,2,1,0:T(8,128)(2,1)}, u32[]{:S(2)}) copy-start(bf16[3,3,3,16,512]{4,3,2,1,0:T(8,128)(2,1)} %param.19) | copy-start | bytes 1327108
  291.8 6.4 %collective-permute-start.1 = (f32[16,3072]{1,0:T(8,128)S(1)}, f32[16,3072]{1,0:T(8,128)S(1)}, u32[]{:S(2)}, u32[]{:S(2)}) collective-permute-start(f32[16,3072]{1,0:T(8,128)S(1)} %fusion.51), channel_id=1, source_target_pairs={{0,1},{1,0},{2,3},{3,2},{4,5},{5,4},{6,7},{7,6},{8,9},{9,8},{10,11... | collective-permute-start | bytes 589832 | tf_op jit(solution)/shard_map/ppermute | solution.py:212
Sparse Core Ops, SparseCore 0:
  30.8 65.8 all-gather.4
